TPU v7x, 32 devices: a whole 2x2x4 slice. The times are simulated.
32 devices in a mesh: row: 4 (over y, x), col: 8 (over z, core).
Axes of the slice: x: 2, y: 2, z: 4, core: 2. Of those that a mesh axis runs over, the one named last changes fastest.
Arguments:
- weights: bfloat16 [3072, 3072], P('col', 'row'), may hold values from -0.109375 to 0.109375
- weight_flags: int32 [24, 24], P('col', 'row'), may hold values from 0 to 1, as said below
- hamiltonian: bfloat16 [3072, 4096], P('row', 'col'), may hold values from -6 to 6
- ham_flags: int32 [24, 32], P('row', 'col'), may hold values from 0 to 1, as said below
Outputs:
- coupling: bfloat16 [3072, 4096], P('row', 'col')
Inputs may be any that keep to these rules, and one draw needn't show every extreme that they name: `weight_flags`: 1 marks a stored block of W, 0 an absent one; the share of stored blocks differs from block row to block row. `ham_flags`: 1 marks a stored block of the slab, 0 an absent one; the share of stored blocks differs from block row to block row.
All inputs are finite; a program needn't handle non-finite values.
Results may differ from a plain program's by a relative error of at most 0.001.
Values may be sent and summed in bfloat16 or wider, within the bound.
A program may use at most 64 MiB of HBM per device.

v0:
```python
import jax
import jax.numpy as jnp
from jax import lax
from jax.sharding import PartitionSpec as P

STEPS = 4


def from_behind(block, axis, distance):
    devices = range(lax.axis_size(axis))
    route = [((i - distance) % len(devices), i) for i in devices]
    return lax.ppermute(block, axis, route)


def from_partner(value, axis, bit):
    mask = 2**bit
    pairs = [(source, source ^ mask) for source in range(lax.axis_size(axis))]
    return lax.ppermute(value, axis, pairs)


def masked(dense_tile, flag_grid):
    row_blocks, col_blocks = flag_grid.shape
    block_edge = dense_tile.shape[0] // row_blocks
    shaped = dense_tile.reshape(row_blocks, block_edge, col_blocks, block_edge)
    retain = (flag_grid > 0)[:, None, :, None]
    return jnp.where(retain, shaped, jnp.zeros_like(shaped)).reshape(dense_tile.shape)


def aligned(operand, amount, bit_count, mover):
    for level in range(bit_count):
        moved = mover(operand, level)
        chosen = (amount >> level) % 2 == 1
        operand = jnp.where(chosen, moved, operand)
    return operand


def contract(left_part, right_part):
    return lax.dot_general(
        left_part, right_part, (((0,), (0,)), ((), ())), preferred_element_type=jnp.float32
    )


def shards(weights, weight_flags, hamiltonian, ham_flags):
    row_count = lax.axis_size("row")
    bit_count = (row_count - 1).bit_length()
    row_index = lax.axis_index("row")
    col_index = lax.axis_index("col")
    pair_index = col_index // 2
    parity = col_index % 2
    w_masked = masked(weights, weight_flags)
    h_masked = masked(hamiltonian, ham_flags)
    ham_tile = aligned(
        h_masked,
        pair_index,
        bit_count,
        lambda operand, level: from_behind(operand, "row", -(1 << level)),
    )
    w_half = aligned(
        w_masked,
        row_index,
        bit_count,
        lambda operand, level: from_behind(operand, "col", -(2 << level)),
    )
    half_rows = ham_tile.shape[0] // 2
    upper_rows = ham_tile[:half_rows]
    lower_rows = ham_tile[half_rows:]
    retained = jnp.where(parity == 0, upper_rows, lower_rows)
    handed = jnp.where(parity == 0, lower_rows, upper_rows)
    received = from_partner(handed, "col", 0)
    joined = jnp.where(
        parity == 0,
        jnp.concatenate((retained, received), 1),
        jnp.concatenate((received, retained), 1),
    )
    summed = contract(w_half, joined)
    for step_index in range(1, STEPS):
        w_half = from_behind(w_half, "col", -2)
        joined = from_behind(joined, "row", -1)
        summed = summed + contract(w_half, joined)
    half_width = summed.shape[1] // 2
    own_part = jnp.where(parity == 0, summed[:, :half_width], summed[:, half_width:])
    their_part = jnp.where(parity == 0, summed[:, half_width:], summed[:, :half_width])
    summed = own_part + from_partner(their_part, "col", 0)
    return summed.astype(jnp.bfloat16)


def solution(mesh):
    placed = (P("col", "row"), P("col", "row"), P("row", "col"), P("row", "col"))
    return jax.shard_map(
        shards, mesh=mesh, in_specs=placed, out_specs=P("row", "col"), check_vma=False
    )
```

profile of v0, /device:TPU:1, one launch (start us, length us, event | category | flops | bytes accessed | tf_op | source)
XLA Modules:
  0.0 125.5 jit_solution(11492623967594409352)
XLA Ops:
  0.0 0.0 copy-start.1
  0.0 0.0 copy-start
  0.0 0.7 broadcast_compare_fusion
  0.8 0.1 copy.6
  0.9 0.3 broadcast_in_dim.31
  1.1 1.3 %bitcast_select_fusion = bf16[768,512]{1,0:T(8,128)(2,1)S(1)} fusion(bf16[768,512]{1,0:T(8,128)(2,1)} %param.6, pred[96,8,4,128]{3,2,1,0:T(4,128)(4,1)S(1)} %bitcast.17), kind=kLoop, calls=%fused_computation.2 | loop fusion | flops 393216 | bytes 1966080 | tf_op jit(solution)/shard_map/jit(_where)/select_n | solution.py:26
  2.5 3.0 %collective-permute-start.2 = (bf16[768,512]{1,0:T(8,128)(2,1)S(1)}, bf16[768,512]{1,0:T(8,128)(2,1)S(1)}, u32[]{:S(2)}, u32[]{:S(2)}) collective-permute-start(bf16[768,512]{1,0:T(8,128)(2,1)S(1)} %bitcast_select_fusion), channel_id=1, source_target_pairs={{8,0},{16,8},{24,16},{0,24},{9,1},{17,9},{25,17},{1,25},{10,2},{18... | collective-permute-start | bytes 2359304 | tf_op jit(solution)/shard_map/ppermute | solution.py:12
  5.5 16.3 %collective-permute-done.2 = bf16[768,512]{1,0:T(8,128)(2,1)S(1)} collective-permute-done((bf16[768,512]{1,0:T(8,128)(2,1)S(1)}, bf16[768,512]{1,0:T(8,128)(2,1)S(1)}, u32[]{:S(2)}, u32[]{:S(2)}) %collective-permute-start.2) | collective-permute-done | bytes 786464 | tf_op jit(solution)/shard_map/ppermute | solution.py:12
  21.8 0.1 broadcast_select_fusion
  21.9 1.3 %collective-permute-start.3 = (bf16[768,512]{1,0:T(8,128)(2,1)S(1)}, bf16[768,512]{1,0:T(8,128)(2,1)S(1)}, u32[]{:S(2)}, u32[]{:S(2)}) collective-permute-start(bf16[768,512]{1,0:T(8,128)(2,1)S(1)} %broadcast_select_fusion), channel_id=1, source_target_pairs={{16,0},{24,8},{0,16},{8,24},{17,1},{25,9},{1,17},{9,25},{18,2},{26... | collective-permute-start | bytes 2359304 | tf_op jit(solution)/shard_map/ppermute | solution.py:12
  23.2 0.0 copy-done.1
  23.2 0.2 broadcast_in_dim.28
  23.4 0.0 copy-done
  23.4 0.2 bitcast_select_fusion.1
  23.5 3.4 %collective-permute-start = (bf16[384,768]{1,0:T(8,128)(2,1)S(1)}, bf16[384,768]{1,0:T(8,128)(2,1)S(1)}, u32[]{:S(2)}, u32[]{:S(2)}) collective-permute-start(bf16[384,768]{1,0:T(8,128)(2,1)S(1)} %bitcast_select_fusion.1), channel_id=1, source_target_pairs={{2,0},{3,1},{4,2},{5,3},{6,4},{7,5},{0,6},{1,7},{10,8},{11,9},{12,... | collective-permute-start | bytes 1769480 | tf_op jit(solution)/shard_map/ppermute | solution.py:12
  26.9 12.7 %collective-permute-done.3 = bf16[768,512]{1,0:T(8,128)(2,1)S(1)} collective-permute-done((bf16[768,512]{1,0:T(8,128)(2,1)S(1)}, bf16[768,512]{1,0:T(8,128)(2,1)S(1)}, u32[]{:S(2)}, u32[]{:S(2)}) %collective-permute-start.3) | collective-permute-done | bytes 786464 | tf_op jit(solution)/shard_map/ppermute | solution.py:12
  39.6 0.1 broadcast_select_fusion.1
  39.7 0.1 broadcast_select_fusion.5
  39.8 2.4 %collective-permute-start.4 = (bf16[384,512]{1,0:T(8,128)(2,1)S(1)}, bf16[384,512]{1,0:T(8,128)(2,1)S(1)}, u32[]{:S(2)}, u32[]{:S(2)}) collective-permute-start(bf16[384,512]{1,0:T(8,128)(2,1)S(1)} %get-tuple-element.6), channel_id=1, source_target_pairs={{0,1},{1,0},{2,3},{3,2},{4,5},{5,4},{6,7},{7,6},{8,9},{9,8},{10,11... | collective-permute-start | bytes 1179656 | tf_op jit(solution)/shard_map/ppermute | solution.py:18
  42.1 0.0 collective-permute-done
  42.1 0.1 broadcast_select_fusion.2
  42.2 2.3 %collective-permute-start.1 = (bf16[384,768]{1,0:T(8,128)(2,1)S(1)}, bf16[384,768]{1,0:T(8,128)(2,1)S(1)}, u32[]{:S(2)}, u32[]{:S(2)}) collective-permute-start(bf16[384,768]{1,0:T(8,128)(2,1)S(1)} %broadcast_select_fusion.2), channel_id=1, source_target_pairs={{4,0},{5,1},{6,2},{7,3},{0,4},{1,5},{2,6},{3,7},{12,8},{13,9},{14,... | collective-permute-start | bytes 1769480 | tf_op jit(solution)/shard_map/ppermute | solution.py:12
  44.6 0.0 collective-permute-done.4
  44.6 0.2 maximum_select_fusion
  44.8 3.1 %collective-permute-start.6 = (bf16[384,1024]{1,0:T(8,128)(2,1)S(1)}, bf16[384,1024]{1,0:T(8,128)(2,1)S(1)}, u32[]{:S(2)}, u32[]{:S(2)}) collective-permute-start(bf16[384,1024]{1,0:T(8,128)(2,1)S(1)} %maximum_select_fusion), channel_id=1, source_target_pairs={{8,0},{16,8},{24,16},{0,24},{9,1},{17,9},{25,17},{1,25},{10,2},{18... | collective-permute-start | bytes 2359304 | tf_op jit(solution)/shard_map/ppermute | solution.py:12
  47.9 22.8 %collective-permute-done.1 = bf16[384,768]{1,0:T(8,128)(2,1)S(1)} collective-permute-done((bf16[384,768]{1,0:T(8,128)(2,1)S(1)}, bf16[384,768]{1,0:T(8,128)(2,1)S(1)}, u32[]{:S(2)}, u32[]{:S(2)}) %collective-permute-start.1) | collective-permute-done | bytes 589856 | tf_op jit(solution)/shard_map/ppermute | solution.py:12
  70.7 0.1 broadcast_select_fusion.3
  70.7 3.7 %collective-permute-start.5 = (bf16[384,768]{1,0:T(8,128)(2,1)S(1)}, bf16[384,768]{1,0:T(8,128)(2,1)S(1)}, u32[]{:S(2)}, u32[]{:S(2)}) collective-permute-start(bf16[384,768]{1,0:T(8,128)(2,1)S(1)} %broadcast_select_fusion.3), channel_id=1, source_target_pairs={{2,0},{3,1},{4,2},{5,3},{6,4},{7,5},{0,6},{1,7},{10,8},{11,9},{12,... | collective-permute-start | bytes 1769480 | tf_op jit(solution)/shard_map/ppermute | solution.py:12
  74.4 0.0 collective-permute-done.6
  74.4 3.1 %collective-permute-start.8 = (bf16[384,1024]{1,0:T(8,128)(2,1)S(1)}, bf16[384,1024]{1,0:T(8,128)(2,1)S(1)}, u32[]{:S(2)}, u32[]{:S(2)}) collective-permute-start(bf16[384,1024]{1,0:T(8,128)(2,1)S(1)} %collective-permute-done.6), channel_id=1, source_target_pairs={{8,0},{16,8},{24,16},{0,24},{9,1},{17,9},{25,17},{1,25},{10,2},{18... | collective-permute-start | bytes 2359304 | tf_op jit(solution)/shard_map/ppermute | solution.py:12
  77.5 9.2 %collective-permute-done.5 = bf16[384,768]{1,0:T(8,128)(2,1)S(1)} collective-permute-done((bf16[384,768]{1,0:T(8,128)(2,1)S(1)}, bf16[384,768]{1,0:T(8,128)(2,1)S(1)}, u32[]{:S(2)}, u32[]{:S(2)}) %collective-permute-start.5) | collective-permute-done | bytes 589856 | tf_op jit(solution)/shard_map/ppermute | solution.py:12
  86.7 4.0 %collective-permute-start.7 = (bf16[384,768]{1,0:T(8,128)(2,1)S(1)}, bf16[384,768]{1,0:T(8,128)(2,1)S(1)}, u32[]{:S(2)}, u32[]{:S(2)}) collective-permute-start(bf16[384,768]{1,0:T(8,128)(2,1)S(1)} %collective-permute-done.5), channel_id=1, source_target_pairs={{2,0},{3,1},{4,2},{5,3},{6,4},{7,5},{0,6},{1,7},{10,8},{11,9},{12,... | collective-permute-start | bytes 1769480 | tf_op jit(solution)/shard_map/ppermute | solution.py:12
  90.7 3.1 %collective-permute-done.8 = bf16[384,1024]{1,0:T(8,128)(2,1)S(1)} collective-permute-done((bf16[384,1024]{1,0:T(8,128)(2,1)S(1)}, bf16[384,1024]{1,0:T(8,128)(2,1)S(1)}, u32[]{:S(2)}, u32[]{:S(2)}) %collective-permute-start.8) | collective-permute-done | bytes 786464 | tf_op jit(solution)/shard_map/ppermute | solution.py:12
  93.7 3.0 %collective-permute-start.10 = (bf16[384,1024]{1,0:T(8,128)(2,1)S(1)}, bf16[384,1024]{1,0:T(8,128)(2,1)S(1)}, u32[]{:S(2)}, u32[]{:S(2)}) collective-permute-start(bf16[384,1024]{1,0:T(8,128)(2,1)S(1)} %collective-permute-done.8), channel_id=1, source_target_pairs={{8,0},{16,8},{24,16},{0,24},{9,1},{17,9},{25,17},{1,25},{10,2},{18... | collective-permute-start | bytes 2359304 | tf_op jit(solution)/shard_map/ppermute | solution.py:12
  96.8 1.0 fusion
  97.8 4.3 %collective-permute-done.7 = bf16[384,768]{1,0:T(8,128)(2,1)S(1)} collective-permute-done((bf16[384,768]{1,0:T(8,128)(2,1)S(1)}, bf16[384,768]{1,0:T(8,128)(2,1)S(1)}, u32[]{:S(2)}, u32[]{:S(2)}) %collective-permute-start.7) | collective-permute-done | bytes 589856 | tf_op jit(solution)/shard_map/ppermute | solution.py:12
  102.0 4.0 %collective-permute-start.9 = (bf16[384,768]{1,0:T(8,128)(2,1)S(1)}, bf16[384,768]{1,0:T(8,128)(2,1)S(1)}, u32[]{:S(2)}, u32[]{:S(2)}) collective-permute-start(bf16[384,768]{1,0:T(8,128)(2,1)S(1)} %collective-permute-done.7), channel_id=1, source_target_pairs={{2,0},{3,1},{4,2},{5,3},{6,4},{7,5},{0,6},{1,7},{10,8},{11,9},{12,... | collective-permute-start | bytes 1769480 | tf_op jit(solution)/shard_map/ppermute | solution.py:12
  106.0 1.0 fusion.1
  107.1 1.0 fusion.2
  108.1 8.5 %collective-permute-done.9 = bf16[384,768]{1,0:T(8,128)(2,1)S(1)} collective-permute-done((bf16[384,768]{1,0:T(8,128)(2,1)S(1)}, bf16[384,768]{1,0:T(8,128)(2,1)S(1)}, u32[]{:S(2)}, u32[]{:S(2)}) %collective-permute-start.9) | collective-permute-done | bytes 589856 | tf_op jit(solution)/shard_map/ppermute | solution.py:12
  116.6 0.0 collective-permute-done.10
  116.6 1.1 add_add_fusion
  117.7 0.3 slice_select_fusion
  118.0 3.1 %collective-permute-start.11 = (f32[768,512]{1,0:T(8,128)S(1)}, f32[768,512]{1,0:T(8,128)S(1)}, u32[]{:S(2)}, u32[]{:S(2)}) collective-permute-start(f32[768,512]{1,0:T(8,128)S(1)} %slice_select_fusion), channel_id=1, source_target_pairs={{0,1},{1,0},{2,3},{3,2},{4,5},{5,4},{6,7},{7,6},{8,9},{9,8},{10,11... | collective-permute-start | bytes 4718600 | tf_op jit(solution)/shard_map/ppermute | solution.py:18
  121.1 3.0 %collective-permute-done.11 = f32[768,512]{1,0:T(8,128)S(1)} collective-permute-done((f32[768,512]{1,0:T(8,128)S(1)}, f32[768,512]{1,0:T(8,128)S(1)}, u32[]{:S(2)}, u32[]{:S(2)}) %collective-permute-start.11) | collective-permute-done | bytes 1572896 | tf_op jit(solution)/shard_map/ppermute | solution.py:18
  124.1 1.4 %add_convert_fusion = bf16[768,512]{1,0:T(8,128)(2,1)} fusion(f32[768,512]{1,0:T(8,128)S(1)} %collective-permute-done.11, f32[768,1024]{1,0:T(8,128)S(1)} %add_add_fusion, pred[]{:T(512)S(6)} %eq.25), kind=kLoop, calls=%fused_computation.1 | loop fusion | flops 1179648 | bytes 5505025 | tf_op jit(solution)/shard_map/convert_element_type | solution.py:84
  (1 shorter events, 0.0 us)
Async XLA Ops:
  0.0 23.2 %copy-start.1 = (s32[3,6]{1,0:T(4,128)S(1)}, s32[3,6]{1,0:T(4,128)}, u32[]{:S(2)}) copy-start(s32[3,6]{1,0:T(4,128)} %param.5) | copy-start | bytes 220
  0.0 23.4 %copy-start = (bf16[384,768]{1,0:T(8,128)(2,1)S(1)}, bf16[384,768]{1,0:T(8,128)(2,1)}, u32[]{:S(2)}) copy-start(bf16[384,768]{1,0:T(8,128)(2,1)} %param.4) | copy-start | bytes 1769476
  2.5 19.3 %collective-permute-start.2 = (bf16[768,512]{1,0:T(8,128)(2,1)S(1)}, bf16[768,512]{1,0:T(8,128)(2,1)S(1)}, u32[]{:S(2)}, u32[]{:S(2)}) collective-permute-start(bf16[768,512]{1,0:T(8,128)(2,1)S(1)} %bitcast_select_fusion), channel_id=1, source_target_pairs={{8,0},{16,8},{24,16},{0,24},{9,1},{17,9},{25,17},{1,25},{10,2},{18... | collective-permute-start | bytes 2359304 | tf_op jit(solution)/shard_map/ppermute | solution.py:12
  21.9 17.7 %collective-permute-start.3 = (bf16[768,512]{1,0:T(8,128)(2,1)S(1)}, bf16[768,512]{1,0:T(8,128)(2,1)S(1)}, u32[]{:S(2)}, u32[]{:S(2)}) collective-permute-start(bf16[768,512]{1,0:T(8,128)(2,1)S(1)} %broadcast_select_fusion), channel_id=1, source_target_pairs={{16,0},{24,8},{0,16},{8,24},{17,1},{25,9},{1,17},{9,25},{18,2},{26... | collective-permute-start | bytes 2359304 | tf_op jit(solution)/shard_map/ppermute | solution.py:12
  23.5 18.6 %collective-permute-start = (bf16[384,768]{1,0:T(8,128)(2,1)S(1)}, bf16[384,768]{1,0:T(8,128)(2,1)S(1)}, u32[]{:S(2)}, u32[]{:S(2)}) collective-permute-start(bf16[384,768]{1,0:T(8,128)(2,1)S(1)} %bitcast_select_fusion.1), channel_id=1, source_target_pairs={{2,0},{3,1},{4,2},{5,3},{6,4},{7,5},{0,6},{1,7},{10,8},{11,9},{12,... | collective-permute-start | bytes 1769480 | tf_op jit(solution)/shard_map/ppermute | solution.py:12
  39.8 4.8 %collective-permute-start.4 = (bf16[384,512]{1,0:T(8,128)(2,1)S(1)}, bf16[384,512]{1,0:T(8,128)(2,1)S(1)}, u32[]{:S(2)}, u32[]{:S(2)}) collective-permute-start(bf16[384,512]{1,0:T(8,128)(2,1)S(1)} %get-tuple-element.6), channel_id=1, source_target_pairs={{0,1},{1,0},{2,3},{3,2},{4,5},{5,4},{6,7},{7,6},{8,9},{9,8},{10,11... | collective-permute-start | bytes 1179656 | tf_op jit(solution)/shard_map/ppermute | solution.py:18
  42.2 28.5 %collective-permute-start.1 = (bf16[384,768]{1,0:T(8,128)(2,1)S(1)}, bf16[384,768]{1,0:T(8,128)(2,1)S(1)}, u32[]{:S(2)}, u32[]{:S(2)}) collective-permute-start(bf16[384,768]{1,0:T(8,128)(2,1)S(1)} %broadcast_select_fusion.2), channel_id=1, source_target_pairs={{4,0},{5,1},{6,2},{7,3},{0,4},{1,5},{2,6},{3,7},{12,8},{13,9},{14,... | collective-permute-start | bytes 1769480 | tf_op jit(solution)/shard_map/ppermute | solution.py:12
  44.8 29.6 %collective-permute-start.6 = (bf16[384,1024]{1,0:T(8,128)(2,1)S(1)}, bf16[384,1024]{1,0:T(8,128)(2,1)S(1)}, u32[]{:S(2)}, u32[]{:S(2)}) collective-permute-start(bf16[384,1024]{1,0:T(8,128)(2,1)S(1)} %maximum_select_fusion), channel_id=1, source_target_pairs={{8,0},{16,8},{24,16},{0,24},{9,1},{17,9},{25,17},{1,25},{10,2},{18... | collective-permute-start | bytes 2359304 | tf_op jit(solution)/shard_map/ppermute | solution.py:12
  70.7 15.9 %collective-permute-start.5 = (bf16[384,768]{1,0:T(8,128)(2,1)S(1)}, bf16[384,768]{1,0:T(8,128)(2,1)S(1)}, u32[]{:S(2)}, u32[]{:S(2)}) collective-permute-start(bf16[384,768]{1,0:T(8,128)(2,1)S(1)} %broadcast_select_fusion.3), channel_id=1, source_target_pairs={{2,0},{3,1},{4,2},{5,3},{6,4},{7,5},{0,6},{1,7},{10,8},{11,9},{12,... | collective-permute-start | bytes 1769480 | tf_op jit(solution)/shard_map/ppermute | solution.py:12
  74.4 19.3 %collective-permute-start.8 = (bf16[384,1024]{1,0:T(8,128)(2,1)S(1)}, bf16[384,1024]{1,0:T(8,128)(2,1)S(1)}, u32[]{:S(2)}, u32[]{:S(2)}) collective-permute-start(bf16[384,1024]{1,0:T(8,128)(2,1)S(1)} %collective-permute-done.6), channel_id=1, source_target_pairs={{8,0},{16,8},{24,16},{0,24},{9,1},{17,9},{25,17},{1,25},{10,2},{18... | collective-permute-start | bytes 2359304 | tf_op jit(solution)/shard_map/ppermute | solution.py:12
  86.7 15.4 %collective-permute-start.7 = (bf16[384,768]{1,0:T(8,128)(2,1)S(1)}, bf16[384,768]{1,0:T(8,128)(2,1)S(1)}, u32[]{:S(2)}, u32[]{:S(2)}) collective-permute-start(bf16[384,768]{1,0:T(8,128)(2,1)S(1)} %collective-permute-done.5), channel_id=1, source_target_pairs={{2,0},{3,1},{4,2},{5,3},{6,4},{7,5},{0,6},{1,7},{10,8},{11,9},{12,... | collective-permute-start | bytes 1769480 | tf_op jit(solution)/shard_map/ppermute | solution.py:12
  93.7 22.9 %collective-permute-start.10 = (bf16[384,1024]{1,0:T(8,128)(2,1)S(1)}, bf16[384,1024]{1,0:T(8,128)(2,1)S(1)}, u32[]{:S(2)}, u32[]{:S(2)}) collective-permute-start(bf16[384,1024]{1,0:T(8,128)(2,1)S(1)} %collective-permute-done.8), channel_id=1, source_target_pairs={{8,0},{16,8},{24,16},{0,24},{9,1},{17,9},{25,17},{1,25},{10,2},{18... | collective-permute-start | bytes 2359304 | tf_op jit(solution)/shard_map/ppermute | solution.py:12
  102.0 14.5 %collective-permute-start.9 = (bf16[384,768]{1,0:T(8,128)(2,1)S(1)}, bf16[384,768]{1,0:T(8,128)(2,1)S(1)}, u32[]{:S(2)}, u32[]{:S(2)}) collective-permute-start(bf16[384,768]{1,0:T(8,128)(2,1)S(1)} %collective-permute-done.7), channel_id=1, source_target_pairs={{2,0},{3,1},{4,2},{5,3},{6,4},{7,5},{0,6},{1,7},{10,8},{11,9},{12,... | collective-permute-start | bytes 1769480 | tf_op jit(solution)/shard_map/ppermute | solution.py:12
  118.0 6.1 %collective-permute-start.11 = (f32[768,512]{1,0:T(8,128)S(1)}, f32[768,512]{1,0:T(8,128)S(1)}, u32[]{:S(2)}, u32[]{:S(2)}) collective-permute-start(f32[768,512]{1,0:T(8,128)S(1)} %slice_select_fusion), channel_id=1, source_target_pairs={{0,1},{1,0},{2,3},{3,2},{4,5},{5,4},{6,7},{7,6},{8,9},{9,8},{10,11... | collective-permute-start | bytes 4718600 | tf_op jit(solution)/shard_map/ppermute | solution.py:18
where the time goes:
time: 126 us
  waiting for transfers between devices  79.8 us (63%)
  starting transfers between devices  36.4 us (29%)
  other arithmetic  4.51 us (4%)
  matrix products  4.13 us (3%)
    ppermute x10, waiting for transfers between devices, from_behind(): return lax.ppermute(block, axis, route)  76.8 us
    ppermute x10, starting transfers between devices, from_behind(): return lax.ppermute(block, axis, route)  30.9 us
    ppermute x2, starting transfers between devices, from_partner(): return lax.ppermute(value, axis, pairs)  5.47 us
    dot_general x4, matrix products, contract(): lax.dot_general(left_part, right_part, (((0,), (0,)), ((), ())), preferre...  4.13 us
    ppermute x2, waiting for transfers between devices, from_partner(): return lax.ppermute(value, axis, pairs)  3.04 us
  transfers between devices with their start and end apart: 12, of which 8 were waited for; matrix products, arithmetic and copies ran while one was open for 3% of the time, Pallas kernels for 0%

commit v1 on v0

--- a/solution.py
+++ b/solution.py
@@ -1,6 +1,10 @@
+import functools
+
 import jax
 import jax.numpy as jnp
 from jax import lax
+from jax.experimental import pallas as pl
+from jax.experimental.pallas import tpu as pltpu
 from jax.sharding import PartitionSpec as P
 
 STEPS = 4
@@ -84,8 +88,249 @@
     return summed.astype(jnp.bfloat16)
 
 
+CHUNKS = 6
+MESH = pl.DeviceIdType.MESH
+
+
+def put(source, target, sent, landed, device):
+    return pltpu.make_async_remote_copy(
+        src_ref=source,
+        dst_ref=target,
+        send_sem=sent,
+        recv_sem=landed,
+        device_id=device,
+        device_id_type=MESH,
+    )
+
+
+def gather_kernel(
+    panels, w_flags, h_flags, w_ref, h_ref, out_ref, w_buf, h_buf, total,
+    w_landed, up_sent, down_sent, core_sent, h_landed, h_sent,
+):
+    row = lax.axis_index("row")
+    col = lax.axis_index("col")
+    pair = col // 2
+    core = col % 2
+    partner = (row, pair * 2 + 1 - core)
+    above = (row, col + 2)
+    below = (row, col - 2)
+    beside = row + 1 - 2 * (row % 2)
+    across = (row + panels // 2) % panels
+    opposite = (beside + panels // 2) % panels
+    has_above = pair < panels - 1
+    has_below = pair > 0
+
+    barrier = pltpu.get_barrier_semaphore()
+
+    def greet(device):
+        pl.semaphore_signal(barrier, inc=1, device_id=device, device_id_type=MESH)
+
+    greet(partner)
+    greet((beside, col))
+    greet((across, col))
+
+    @pl.when(has_above)
+    def _():
+        greet(above)
+
+    @pl.when(has_below)
+    def _():
+        greet(below)
+
+    chunk_rows, width = w_buf.shape[3], w_buf.shape[4]
+    edge = w_ref.shape[0] // w_flags.shape[0]
+    for k in range(CHUNKS):
+        for c in range(w_flags.shape[1]):
+            lanes = slice(c * edge, (c + 1) * edge)
+            for start in range(k * chunk_rows, (k + 1) * chunk_rows, min(edge, chunk_rows)):
+                rows = slice(start, start + min(edge, chunk_rows))
+                block = w_ref[rows, lanes]
+                keep = w_flags[start // edge, c] > 0
+                inner = slice(start - k * chunk_rows, start - k * chunk_rows + min(edge, chunk_rows))
+                w_buf[pair, core, k, inner, lanes] = jnp.where(keep, block, jnp.zeros_like(block))
+    half_rows = h_buf.shape[2]
+    for r in range(h_flags.shape[0]):
+        for c in range(h_flags.shape[1]):
+            lanes = slice(c * edge, (c + 1) * edge)
+            block = h_ref[r * edge:(r + 1) * edge, lanes]
+            half, start = divmod(r * edge, half_rows)
+            kept = jnp.where(h_flags[r, c] > 0, block, jnp.zeros_like(block))
+            h_buf[row, half, start:start + edge, lanes] = kept
+
+    pl.semaphore_wait(
+        barrier, 3 + has_above.astype(jnp.int32) + has_below.astype(jnp.int32)
+    )
+
+    def go_up(panel, k):
+        slot = w_buf.at[panel, core, k]
+        return put(slot, slot, up_sent.at[panel, k], w_landed.at[panel, core, k], above)
+
+    def go_down(panel, k):
+        slot = w_buf.at[panel, core, k]
+        return put(slot, slot, down_sent.at[panel, k], w_landed.at[panel, core, k], below)
+
+    def go_over(panel, k):
+        slot = w_buf.at[panel, core, k]
+        return put(slot, slot, core_sent.at[panel, k], w_landed.at[panel, core, k], partner)
+
+    def arrival(panel, half, k):
+        slot = w_buf.at[panel, half, k]
+        return put(slot, slot, core_sent.at[panel, k], w_landed.at[panel, half, k], partner)
+
+    def h_put(panel, half, number, device):
+        slot = h_buf.at[panel, half]
+        return put(slot, slot, h_sent.at[number], h_landed.at[panel, half], device)
+
+    def each(body):
+        def step(k, carry):
+            body(k)
+            return carry
+
+        lax.fori_loop(0, CHUNKS, step, 0)
+
+    def first_sends(k):
+        @pl.when(has_above)
+        def _():
+            go_up(pair, k).start()
+
+        @pl.when(has_below)
+        def _():
+            go_down(pair, k).start()
+
+    each(first_sends)
+    h_copies = [
+        h_put(row, 0, 0, (beside, col)),
+        h_put(row, 1, 1, (across, col)),
+        h_put(row, 1, 2, (beside, col)),
+        h_put(row, 0, 3, (across, col)),
+    ]
+    for copy in h_copies:
+        copy.start()
+    each(lambda k: go_over(pair, k).start())
+
+    def relay(distance, k):
+        @pl.when(pair >= distance)
+        def _():
+            panel = pair - distance
+            arrival(panel, core, k).wait_recv()
+
+            @pl.when(has_above)
+            def _():
+                go_up(panel, k).start()
+
+            go_over(panel, k).start()
+
+        @pl.when(pair + distance < panels)
+        def _():
+            panel = pair + distance
+            arrival(panel, core, k).wait_recv()
+
+            @pl.when(has_below)
+            def _():
+                go_down(panel, k).start()
+
+            go_over(panel, k).start()
+
+    each(functools.partial(relay, 1))
+    h_put(beside, 0, 0, (beside, col)).wait_recv()
+    relay_across = h_put(beside, 0, 4, (across, col))
+    relay_across.start()
+    h_put(across, 1, 0, (beside, col)).wait_recv()
+    relay_beside = h_put(across, 1, 5, (beside, col))
+    relay_beside.start()
+    for distance in range(2, panels - 1):
+        each(functools.partial(relay, distance))
+    h_put(beside, 1, 0, (beside, col)).wait_recv()
+    h_put(across, 0, 0, (beside, col)).wait_recv()
+    h_put(opposite, 0, 0, (beside, col)).wait_recv()
+    h_put(opposite, 1, 0, (beside, col)).wait_recv()
+
+    total[...] = jnp.zeros_like(total)
+    span = CHUNKS * chunk_rows
+
+    def near_panel(step, carry):
+        panel = (pair + step) % panels
+        gap = panel - pair
+
+        @pl.when((gap < panels - 1) & (gap > 1 - panels))
+        def _():
+            each(lambda k: arrival(panel, 1 - core, k).wait_recv())
+            left = w_buf[panel].reshape(2 * span, width)
+            right = h_buf[panel].reshape(2 * span, h_buf.shape[3])
+            total[...] += contract(left, right)
+
+        return carry
+
+    lax.fori_loop(0, panels, near_panel, 0)
+
+    @pl.when((pair == 0) | (pair == panels - 1))
+    def _():
+        panel = panels - 1 - pair
+
+        def far_chunk(k):
+            arrival(panel, core, k).wait_recv()
+            go_over(panel, k).start()
+            rows = pl.ds(pl.multiple_of(k * chunk_rows, chunk_rows), chunk_rows)
+            total[...] += contract(w_buf[panel, core, k], h_buf[panel, core, rows, :])
+            arrival(panel, 1 - core, k).wait_recv()
+            total[...] += contract(w_buf[panel, 1 - core, k], h_buf[panel, 1 - core, rows, :])
+
+        each(far_chunk)
+
+    out_ref[...] = total[...].astype(out_ref.dtype)
+
+    for copy in h_copies + [relay_across, relay_beside]:
+        copy.wait_send()
+
+    def drain(panel, carry):
+        def one(k):
+            go_over(panel, k).wait_send()
+
+            @pl.when(has_above & (panel <= pair))
+            def _():
+                go_up(panel, k).wait_send()
+
+            @pl.when(has_below & (panel >= pair))
+            def _():
+                go_down(panel, k).wait_send()
+
+        each(one)
+        return carry
+
+    lax.fori_loop(0, panels, drain, 0)
+
+
+def gathered(weights, weight_flags, hamiltonian, ham_flags):
+    panels = lax.axis_size("row")
+    half_rows, width = weights.shape
+    panel_rows, slice_cols = hamiltonian.shape
+    dma = pltpu.SemaphoreType.DMA
+    vmem = pl.BlockSpec(memory_space=pltpu.VMEM)
+    smem = pl.BlockSpec(memory_space=pltpu.SMEM)
+    return pl.pallas_call(
+        functools.partial(gather_kernel, panels),
+        out_shape=jax.ShapeDtypeStruct((width, slice_cols), jnp.bfloat16),
+        in_specs=[smem, smem, vmem, vmem],
+        out_specs=vmem,
+        scratch_shapes=[
+            pltpu.VMEM((panels, 2, CHUNKS, half_rows // CHUNKS, width), jnp.bfloat16),
+            pltpu.VMEM((panels, 2, panel_rows // 2, slice_cols), jnp.bfloat16),
+            pltpu.VMEM((width, slice_cols), jnp.float32),
+            dma((panels, 2, CHUNKS)),
+            dma((panels, CHUNKS)),
+            dma((panels, CHUNKS)),
+            dma((panels, CHUNKS)),
+            dma((panels, 2)),
+            dma((6,)),
+        ],
+        compiler_params=pltpu.CompilerParams(collective_id=0, has_side_effects=True),
+    )(weight_flags, ham_flags, weights, hamiltonian)
+
+
 def solution(mesh):
     placed = (P("col", "row"), P("col", "row"), P("row", "col"), P("row", "col"))
+    every_panel = mesh.shape["row"] == STEPS and mesh.shape["col"] == 2 * STEPS
     return jax.shard_map(
-        shards, mesh=mesh, in_specs=placed, out_specs=P("row", "col"), check_vma=False
-    )
+        gathered if every_panel else shards,
+        mesh=mesh, in_specs=placed, out_specs=P("row", "col"), check_vma=False,
+    )

time: 126 us -> 52.2 us (0.41)
  waiting for transfers between devices: 79.8 us -> 0 us
  Pallas kernels: 0 us -> 48 us
  starting transfers between devices: 36.4 us -> 0 us
  other arithmetic: 4.51 us -> 0 us
  matrix products: 4.13 us -> 0 us
  local copies, waits for them, and re-layouts: 0.57 us -> 3.42 us
    ppermute x12 -> x0, waiting for transfers between devices: 79.8 us -> none  [the longest x10 76.8 us: from_behind(): return lax.ppermute(block, axis, route)]
    pallas_call x0 -> x1, Pallas kernels: none -> 48 us  [gathered(): pl.pallas_call(functools.partial(gather_kernel, panels), out_shape=jax.Sh...]
    ppermute x12 -> x0, starting transfers between devices: 36.4 us -> none  [the longest x10 30.9 us: from_behind(): return lax.ppermute(block, axis, route)]
    dot_general x4 -> x0, matrix products: 4.13 us -> none  [contract(): lax.dot_general(left_part, right_part, (((0,), (0,)), ((), ())), preferre...]
    unnamed x4 -> x2, local copies, waits for them, and re-layouts: 0.01 us -> 3.42 us
    select_n x9 -> x0, other arithmetic: 2.4 us -> none  [the longest x2 1.5 us: masked(): jnp.where(retain, shaped, jnp.zeros_like(shaped)).reshape(dense_tile.shape)]
    convert_element_type x1 -> x0, other arithmetic: 1.36 us -> none  [shards(): return summed.astype(jnp.bfloat16)]
  transfers between devices with their start and end apart: 12 -> 0, of which waited for: 8 -> 0; matrix products, arithmetic and copies ran while one was open for 3% -> 0% of each run, Pallas kernels for 0% -> 0%
where the time goes in v1:
time: 52.2 us; the launch traced here: 51.4 us
  Pallas kernels  48 us (92%)
  local copies, waits for them, and re-layouts  3.42 us (7%)
    pallas_call x1, Pallas kernels, gathered(): pl.pallas_call(functools.partial(gather_kernel, panels), out_shape=jax.Sh...  48 us
    unnamed x2, local copies, waits for them, and re-layouts  3.42 us

profile of v1, /device:TPU:1, one launch (start us, length us, event | category | flops | bytes accessed | tf_op | source)
XLA Modules:
  0.0 51.4 jit_solution(15915600388428527739)
XLA Ops:
  0.0 1.4 %copy.5.h_flags = s32[6,4]{1,0:T(8,128)} copy(s32[6,4]{0,1:T(4,128)} %param.7) | data formatting | bytes 192 | tf_op args[3]
  1.4 48.0 %shard_map.46 = bf16[768,512]{1,0:T(8,128)(2,1)} custom-call(s32[3,6]{1,0:T(4,128)} %w_flags.1, s32[6,4]{1,0:T(8,128)} %copy.5.h_flags, bf16[384,768]{1,0:T(8,128)(2,1)} %w_ref.1, bf16[768,512]{1,0:T(8,128)(2,1)} %h_ref.1), custom_call_target="tpu_custom_call" | custom-call | tf_op jit(solution)/shard_map/pallas_call | solution.py:310
  49.3 2.1 %copy.7 = bf16[768,512]{1,0:T(8,128)(2,1)} copy(bf16[768,512]{1,0:T(8,128)(2,1)} %shard_map.46) | data formatting | bytes 1572864

commit v2 on v1

--- a/solution.py
+++ b/solution.py
@@ -88,7 +88,8 @@
     return summed.astype(jnp.bfloat16)
 
 
-CHUNKS = 6
+SHARES = (1, 1, 1)
+CHUNKS = len(SHARES)
 MESH = pl.DeviceIdType.MESH
 
 
@@ -104,8 +105,8 @@
 
 
 def gather_kernel(
-    panels, w_flags, h_flags, w_ref, h_ref, out_ref, w_buf, h_buf, total,
-    w_landed, up_sent, down_sent, core_sent, h_landed, h_sent,
+    panels, w_flags_hbm, h_flags_hbm, w_hbm, h_hbm, out_ref, w_flags, h_flags, w_ref, h_ref, w_buf, h_buf, total,
+    loaded, w_landed, up_sent, down_sent, core_sent, h_landed, h_sent,
 ):
     row = lax.axis_index("row")
     col = lax.axis_index("col")
@@ -120,6 +121,15 @@
     has_above = pair < panels - 1
     has_below = pair > 0
 
+    loads = [
+        pltpu.make_async_copy(source, target, loaded.at[n])
+        for n, (source, target) in enumerate(
+            ((w_flags_hbm, w_flags), (w_hbm, w_ref), (h_flags_hbm, h_flags), (h_hbm, h_ref))
+        )
+    ]
+    for load in loads:
+        load.start()
+
     barrier = pltpu.get_barrier_semaphore()
 
     def greet(device):
@@ -137,44 +147,48 @@
     def _():
         greet(below)
 
-    chunk_rows, width = w_buf.shape[3], w_buf.shape[4]
-    edge = w_ref.shape[0] // w_flags.shape[0]
-    for k in range(CHUNKS):
+    loads[0].wait()
+    loads[1].wait()
+    half_rows, width = w_ref.shape
+    edge = half_rows // w_flags.shape[0]
+    bounds = [half_rows * sum(SHARES[:k]) // sum(SHARES) for k in range(CHUNKS + 1)]
+    for r in range(w_flags.shape[0]):
         for c in range(w_flags.shape[1]):
-            lanes = slice(c * edge, (c + 1) * edge)
-            for start in range(k * chunk_rows, (k + 1) * chunk_rows, min(edge, chunk_rows)):
-                rows = slice(start, start + min(edge, chunk_rows))
-                block = w_ref[rows, lanes]
-                keep = w_flags[start // edge, c] > 0
-                inner = slice(start - k * chunk_rows, start - k * chunk_rows + min(edge, chunk_rows))
-                w_buf[pair, core, k, inner, lanes] = jnp.where(keep, block, jnp.zeros_like(block))
-    half_rows = h_buf.shape[2]
-    for r in range(h_flags.shape[0]):
-        for c in range(h_flags.shape[1]):
+            rows, lanes = slice(r * edge, (r + 1) * edge), slice(c * edge, (c + 1) * edge)
+            block = w_ref[rows, lanes]
+            kept = jnp.where(w_flags[r, c] > 0, block, jnp.zeros_like(block))
+            w_buf[pair, core, rows, lanes] = kept
+    loads[2].wait()
+    loads[3].wait()
+    for r in range(h_flags.shape[1]):
+        for c in range(h_flags.shape[0]):
             lanes = slice(c * edge, (c + 1) * edge)
             block = h_ref[r * edge:(r + 1) * edge, lanes]
             half, start = divmod(r * edge, half_rows)
-            kept = jnp.where(h_flags[r, c] > 0, block, jnp.zeros_like(block))
+            kept = jnp.where(h_flags[c, r] > 0, block, jnp.zeros_like(block))
             h_buf[row, half, start:start + edge, lanes] = kept
 
     pl.semaphore_wait(
         barrier, 3 + has_above.astype(jnp.int32) + has_below.astype(jnp.int32)
     )
 
+    def piece(k):
+        return slice(bounds[k], bounds[k + 1])
+
     def go_up(panel, k):
-        slot = w_buf.at[panel, core, k]
+        slot = w_buf.at[panel, core, piece(k)]
         return put(slot, slot, up_sent.at[panel, k], w_landed.at[panel, core, k], above)
 
     def go_down(panel, k):
-        slot = w_buf.at[panel, core, k]
+        slot = w_buf.at[panel, core, piece(k)]
         return put(slot, slot, down_sent.at[panel, k], w_landed.at[panel, core, k], below)
 
     def go_over(panel, k):
-        slot = w_buf.at[panel, core, k]
+        slot = w_buf.at[panel, core, piece(k)]
         return put(slot, slot, core_sent.at[panel, k], w_landed.at[panel, core, k], partner)
 
     def arrival(panel, half, k):
-        slot = w_buf.at[panel, half, k]
+        slot = w_buf.at[panel, half, piece(k)]
         return put(slot, slot, core_sent.at[panel, k], w_landed.at[panel, half, k], partner)
 
     def h_put(panel, half, number, device):
@@ -182,11 +196,8 @@
         return put(slot, slot, h_sent.at[number], h_landed.at[panel, half], device)
 
     def each(body):
-        def step(k, carry):
+        for k in range(CHUNKS):
             body(k)
-            return carry
-
-        lax.fori_loop(0, CHUNKS, step, 0)
 
     def first_sends(k):
         @pl.when(has_above)
@@ -246,7 +257,7 @@
     h_put(opposite, 1, 0, (beside, col)).wait_recv()
 
     total[...] = jnp.zeros_like(total)
-    span = CHUNKS * chunk_rows
+    span = 2 * half_rows
 
     def near_panel(step, carry):
         panel = (pair + step) % panels
@@ -255,29 +266,40 @@
         @pl.when((gap < panels - 1) & (gap > 1 - panels))
         def _():
             each(lambda k: arrival(panel, 1 - core, k).wait_recv())
-            left = w_buf[panel].reshape(2 * span, width)
-            right = h_buf[panel].reshape(2 * span, h_buf.shape[3])
+            left = w_buf[panel].reshape(span, width)
+            right = h_buf[panel].reshape(span, h_buf.shape[3])
             total[...] += contract(left, right)
 
         return carry
 
     lax.fori_loop(0, panels, near_panel, 0)
 
-    @pl.when((pair == 0) | (pair == panels - 1))
+    is_end = (pair == 0) | (pair == panels - 1)
+
+    @pl.when(is_end)
     def _():
         panel = panels - 1 - pair
 
-        def far_chunk(k):
+        def product(half, k):
+            return contract(w_buf[panel, half, piece(k)], h_buf[panel, half, piece(k)])
+
+        for k in range(CHUNKS - 1):
             arrival(panel, core, k).wait_recv()
             go_over(panel, k).start()
-            rows = pl.ds(pl.multiple_of(k * chunk_rows, chunk_rows), chunk_rows)
-            total[...] += contract(w_buf[panel, core, k], h_buf[panel, core, rows, :])
+            total[...] += product(core, k)
             arrival(panel, 1 - core, k).wait_recv()
-            total[...] += contract(w_buf[panel, 1 - core, k], h_buf[panel, 1 - core, rows, :])
-
-        each(far_chunk)
-
-    out_ref[...] = total[...].astype(out_ref.dtype)
+            total[...] += product(1 - core, k)
+
+        last = CHUNKS - 1
+        arrival(panel, core, last).wait_recv()
+        go_over(panel, last).start()
+        total[...] += product(core, last)
+        arrival(panel, 1 - core, last).wait_recv()
+        out_ref[...] = (total[...] + product(1 - core, last)).astype(out_ref.dtype)
+
+    @pl.when(jnp.logical_not(is_end))
+    def _():
+        out_ref[...] = total[...].astype(out_ref.dtype)
 
     for copy in h_copies + [relay_across, relay_beside]:
         copy.wait_send()
@@ -306,16 +328,21 @@
     panel_rows, slice_cols = hamiltonian.shape
     dma = pltpu.SemaphoreType.DMA
     vmem = pl.BlockSpec(memory_space=pltpu.VMEM)
-    smem = pl.BlockSpec(memory_space=pltpu.SMEM)
+    hbm = pl.BlockSpec(memory_space=pl.ANY)
     return pl.pallas_call(
         functools.partial(gather_kernel, panels),
-        out_shape=jax.ShapeDtypeStruct((width, slice_cols), jnp.bfloat16),
-        in_specs=[smem, smem, vmem, vmem],
+        out_shape=pltpu.VMEM((width, slice_cols), jnp.bfloat16),
+        in_specs=[hbm] * 4,
         out_specs=vmem,
         scratch_shapes=[
-            pltpu.VMEM((panels, 2, CHUNKS, half_rows // CHUNKS, width), jnp.bfloat16),
+            pltpu.SMEM(weight_flags.shape, weight_flags.dtype),
+            pltpu.SMEM(ham_flags.shape[::-1], ham_flags.dtype),
+            pltpu.VMEM(weights.shape, weights.dtype),
+            pltpu.VMEM(hamiltonian.shape, hamiltonian.dtype),
+            pltpu.VMEM((panels, 2, half_rows, width), jnp.bfloat16),
             pltpu.VMEM((panels, 2, panel_rows // 2, slice_cols), jnp.bfloat16),
             pltpu.VMEM((width, slice_cols), jnp.float32),
+            dma((4,)),
             dma((panels, 2, CHUNKS)),
             dma((panels, CHUNKS)),
             dma((panels, CHUNKS)),
@@ -324,7 +351,7 @@
             dma((6,)),
         ],
         compiler_params=pltpu.CompilerParams(collective_id=0, has_side_effects=True),
-    )(weight_flags, ham_flags, weights, hamiltonian)
+    )(weight_flags, ham_flags.T, weights, hamiltonian)
 
 
 def solution(mesh):

time: 52.2 us -> 46.3 us (0.89); the launches traced: 51.4 us -> 46.2 us
  Pallas kernels: 48 us -> 45.3 us
  local copies, waits for them, and re-layouts: 3.42 us -> 0.88 us
    pallas_call x1, Pallas kernels: 48 us -> 45.3 us  [gathered(): pl.pallas_call(functools.partial(gather_kernel, panels), out_shape=pltpu....]
    unnamed x2 -> x1, local copies, waits for them, and re-layouts: 3.42 us -> 0.88 us
where the time goes in v2:
time: 46.3 us; the launch traced here: 46.2 us
  Pallas kernels  45.3 us (98%)
  local copies, waits for them, and re-layouts  0.88 us (2%)
    pallas_call x1, Pallas kernels, gathered(): pl.pallas_call(functools.partial(gather_kernel, panels), out_shape=pltpu....  45.3 us

profile of v2, /device:TPU:1, one launch (start us, length us, event | category | flops | bytes accessed | tf_op | source)
XLA Modules:
  0.0 46.2 jit_solution(3657117573615736389)
XLA Ops:
  0.0 45.3 %shard_map.46 = bf16[768,512]{1,0:T(8,128)(2,1)S(1)} custom-call(s32[3,6]{1,0:T(4,128)} %w_flags_hbm.1, s32[4,6]{1,0:T(4,128)} %bitcast.1, bf16[384,768]{1,0:T(8,128)(2,1)} %w_hbm.1, bf16[768,512]{1,0:T(8,128)(2,1)} %h_hbm.1), custom_call_target="tpu_custom_call" | custom-call | tf_op jit(solution)/shard_map/pallas_call | solution.py:332
  45.3 0.9 %copy.6 = bf16[768,512]{1,0:T(8,128)(2,1)} copy(bf16[768,512]{1,0:T(8,128)(2,1)S(1)} %shard_map.46) | data formatting | bytes 1572864

commit v3 on v2

--- a/solution.py
+++ b/solution.py
@@ -158,6 +158,47 @@
             block = w_ref[rows, lanes]
             kept = jnp.where(w_flags[r, c] > 0, block, jnp.zeros_like(block))
             w_buf[pair, core, rows, lanes] = kept
+    pl.semaphore_wait(
+        barrier, 3 + has_above.astype(jnp.int32) + has_below.astype(jnp.int32)
+    )
+
+    def piece(k):
+        return slice(bounds[k], bounds[k + 1])
+
+    def go_up(panel, k):
+        slot = w_buf.at[panel, core, piece(k)]
+        return put(slot, slot, up_sent.at[panel, k], w_landed.at[panel, core, k], above)
+
+    def go_down(panel, k):
+        slot = w_buf.at[panel, core, piece(k)]
+        return put(slot, slot, down_sent.at[panel, k], w_landed.at[panel, core, k], below)
+
+    def go_over(panel, k):
+        slot = w_buf.at[panel, core, piece(k)]
+        return put(slot, slot, core_sent.at[panel, k], w_landed.at[panel, core, k], partner)
+
+    def arrival(panel, half, k):
+        slot = w_buf.at[panel, half, piece(k)]
+        return put(slot, slot, core_sent.at[panel, k], w_landed.at[panel, half, k], partner)
+
+    def h_put(panel, half, number, device):
+        slot = h_buf.at[panel, half]
+        return put(slot, slot, h_sent.at[number], h_landed.at[panel, half], device)
+
+    def each(body):
+        for k in range(CHUNKS):
+            body(k)
+
+    def first_sends(k):
+        @pl.when(has_above)
+        def _():
+            go_up(pair, k).start()
+
+        @pl.when(has_below)
+        def _():
+            go_down(pair, k).start()
+
+    each(first_sends)
     loads[2].wait()
     loads[3].wait()
     for r in range(h_flags.shape[1]):
@@ -168,47 +209,6 @@
             kept = jnp.where(h_flags[c, r] > 0, block, jnp.zeros_like(block))
             h_buf[row, half, start:start + edge, lanes] = kept
 
-    pl.semaphore_wait(
-        barrier, 3 + has_above.astype(jnp.int32) + has_below.astype(jnp.int32)
-    )
-
-    def piece(k):
-        return slice(bounds[k], bounds[k + 1])
-
-    def go_up(panel, k):
-        slot = w_buf.at[panel, core, piece(k)]
-        return put(slot, slot, up_sent.at[panel, k], w_landed.at[panel, core, k], above)
-
-    def go_down(panel, k):
-        slot = w_buf.at[panel, core, piece(k)]
-        return put(slot, slot, down_sent.at[panel, k], w_landed.at[panel, core, k], below)
-
-    def go_over(panel, k):
-        slot = w_buf.at[panel, core, piece(k)]
-        return put(slot, slot, core_sent.at[panel, k], w_landed.at[panel, core, k], partner)
-
-    def arrival(panel, half, k):
-        slot = w_buf.at[panel, half, piece(k)]
-        return put(slot, slot, core_sent.at[panel, k], w_landed.at[panel, half, k], partner)
-
-    def h_put(panel, half, number, device):
-        slot = h_buf.at[panel, half]
-        return put(slot, slot, h_sent.at[number], h_landed.at[panel, half], device)
-
-    def each(body):
-        for k in range(CHUNKS):
-            body(k)
-
-    def first_sends(k):
-        @pl.when(has_above)
-        def _():
-            go_up(pair, k).start()
-
-        @pl.when(has_below)
-        def _():
-            go_down(pair, k).start()
-
-    each(first_sends)
     h_copies = [
         h_put(row, 0, 0, (beside, col)),
         h_put(row, 1, 1, (across, col)),

time: 46.3 us -> 46.1 us (level)
  no operation moved by 1% of the time
where the time goes in v3:
time: 46.1 us; the launch traced here: 46 us
  Pallas kernels  45.1 us (98%)
  local copies, waits for them, and re-layouts  0.88 us (2%)
    pallas_call x1, Pallas kernels, gathered(): pl.pallas_call(functools.partial(gather_kernel, panels), out_shape=pltpu....  45.1 us

profile of v3, /device:TPU:1, one launch (start us, length us, event | category | flops | bytes accessed | tf_op | source)
XLA Modules:
  0.0 46.0 jit_solution(13261893168649669109)
XLA Ops:
  0.0 45.1 %shard_map.46 = bf16[768,512]{1,0:T(8,128)(2,1)S(1)} custom-call(s32[3,6]{1,0:T(4,128)} %w_flags_hbm.1, s32[4,6]{1,0:T(4,128)} %bitcast.1, bf16[384,768]{1,0:T(8,128)(2,1)} %w_hbm.1, bf16[768,512]{1,0:T(8,128)(2,1)} %h_hbm.1), custom_call_target="tpu_custom_call" | custom-call | tf_op jit(solution)/shard_map/pallas_call | solution.py:332
  45.1 0.9 %copy.6 = bf16[768,512]{1,0:T(8,128)(2,1)} copy(bf16[768,512]{1,0:T(8,128)(2,1)S(1)} %shard_map.46) | data formatting | bytes 1572864

commit v4 on v3

--- a/solution.py
+++ b/solution.py
@@ -88,7 +88,7 @@
     return summed.astype(jnp.bfloat16)
 
 
-SHARES = (1, 1, 1)
+SHARES = (5, 3)
 CHUNKS = len(SHARES)
 MESH = pl.DeviceIdType.MESH
 

time: 46.1 us -> 46 us (level)
  no operation moved by 1% of the time
where the time goes in v4:
time: 46 us; the launch traced here: 45.8 us
  Pallas kernels  44.9 us (98%)
  local copies, waits for them, and re-layouts  0.88 us (2%)
    pallas_call x1, Pallas kernels, gathered(): pl.pallas_call(functools.partial(gather_kernel, panels), out_shape=pltpu....  44.9 us

profile of v4, /device:TPU:1, one launch (start us, length us, event | category | flops | bytes accessed | tf_op | source)
XLA Modules:
  0.0 45.8 jit_solution(4442482580952085528)
XLA Ops:
  0.0 44.9 %shard_map.46 = bf16[768,512]{1,0:T(8,128)(2,1)S(1)} custom-call(s32[3,6]{1,0:T(4,128)} %w_flags_hbm.1, s32[4,6]{1,0:T(4,128)} %bitcast.1, bf16[384,768]{1,0:T(8,128)(2,1)} %w_hbm.1, bf16[768,512]{1,0:T(8,128)(2,1)} %h_hbm.1), custom_call_target="tpu_custom_call" | custom-call | tf_op jit(solution)/shard_map/pallas_call | solution.py:332
  44.9 0.9 %copy.6 = bf16[768,512]{1,0:T(8,128)(2,1)} copy(bf16[768,512]{1,0:T(8,128)(2,1)S(1)} %shard_map.46) | data formatting | bytes 1572864
